TPU v7x, 256 devices: a whole 4x4x8 slice. The times are simulated.
256 devices in a mesh: dp: 16 (over y_lo, z), fsdp: 16 (over x, y_hi, core).
Axes of the slice: x: 4, y: 4 (y_hi: 2, y_lo: 2; y = y_hi * 2 + y_lo), z: 8, core: 2. Of those that a mesh axis runs over, the one named last changes fastest.
Arguments:
- frames: bfloat16 [256, 256, 1536], P(('dp', 'fsdp')), may hold values from -6 to 6
- cotangent: bfloat16 [256, 256, 1536], P(('dp', 'fsdp')), may hold values from -6 to 6
- lengths: int32 [256], P(('dp', 'fsdp')), may hold values from 64 to 256, as said below
- weight_slots: bfloat16 [2304, 3072], P('fsdp'), may hold values from -0.15625 to 0.15625
- owner_rows: int32 [2304], replicated, may hold values from -1 to 1535, as said below
- gain_in: float32 [1536], replicated, may hold values from 0.5 to 1.5
- gain_mid: float32 [1536], replicated, may hold values from 0.5 to 1.5
- kernel: float32 [32, 1536], replicated, may hold values from -1 to 1
Outputs:
- frame_grads: bfloat16 [256, 256, 1536], P(('dp', 'fsdp'))
- weight_grads: bfloat16 [2304, 3072], P('fsdp')
- gain_in_grad: float32 [1536], replicated
- gain_mid_grad: float32 [1536], replicated
- kernel_grad: float32 [32, 1536], replicated
Inputs may be any that keep to these rules, and one draw needn't show every extreme that they name: `owner_rows`: slots o * 144 to o * 144 + 143 belong to owner o (index o of fsdp): first the rows it holds, then -1. Each of the 1536 rows is named by exactly one slot. An owner holds between 48 and 144 rows, and some owner holds exactly 144. Rows of weight_slots in slots marked -1 are not used. `lengths`: some utterance has all 256 frames in use.
All inputs are finite; a program needn't handle non-finite values.
Results may differ from a plain program's by a relative error of at most 0.02.
Values may be sent and summed in bfloat16 or wider, within the bound.
A program may use at most 192 MiB of HBM per device.

v0:
```python
import jax
import jax.numpy as jnp
from jax import lax
from jax.sharding import PartitionSpec as P

EPSILON = 1e-05


def norm_rows(values, scales):
    row_mean = jnp.mean(values, axis=-1, keepdims=True)
    centred = values - row_mean
    spread = jnp.mean(centred * centred, axis=-1, keepdims=True)
    return centred * lax.rsqrt(spread + EPSILON) * scales


def branch_tail(projected, gain_mid, kernel, frame_keep):
    features = gain_mid.shape[0]
    kernel_taps = kernel.shape[0]
    gated = (
        projected[..., :features]
        * jax.nn.sigmoid(projected[..., features:])
        * frame_keep[..., None]
    )
    length = gated.shape[1]
    left_pad = kernel_taps // 2
    padded = jnp.pad(gated, ((0, 0), (left_pad, kernel_taps - 1 - left_pad), (0, 0)))
    convolved = jnp.zeros_like(gated)
    for offset in range(kernel_taps):
        convolved = convolved + kernel[offset] * padded[:, offset : offset + length, :]
    mixed = norm_rows(convolved, gain_mid)
    return mixed * jax.nn.sigmoid(mixed) * frame_keep[..., None]


def per_device(frames, cotangent, lengths, weight_slots, owner_rows, gain_in, gain_mid, kernel):
    utterances, length, features = frames.shape
    token_rows = utterances * length
    slot_count = owner_rows.shape[0]
    valid_slot = owner_rows >= 0
    safe_rows = jnp.where(valid_slot, owner_rows, 0)
    valid_mask = valid_slot.astype(jnp.bfloat16)
    frame_keep = (jnp.arange(length)[None, :] < lengths[:, None]).astype(jnp.float32)
    frames_wide = frames.astype(jnp.float32)
    normed, head_back = jax.vjp(norm_rows, frames_wide, gain_in)
    normed_flat = normed.astype(jnp.bfloat16).reshape(token_rows, features)
    gathered = lax.all_gather(weight_slots, "fsdp", axis=0, tiled=True)
    inverse = (
        jnp.zeros((features,), jnp.int32)
        .at[jnp.where(valid_slot, owner_rows, features)]
        .set(jnp.arange(slot_count, dtype=jnp.int32), mode="drop")
    )
    weight = jnp.take(gathered, inverse, axis=0)
    projected = jnp.dot(normed_flat, weight, preferred_element_type=jnp.float32)
    projected = projected.reshape(utterances, length, 2 * features)
    cotangent_wide = cotangent.astype(jnp.float32)

    def run_tail(projected_in, mid_scales, taps_in):
        return branch_tail(projected_in, mid_scales, taps_in, frame_keep)

    branch, tail_back = jax.vjp(run_tail, projected, gain_mid, kernel)
    projected_grad, gain_mid_grad, kernel_grad = tail_back(cotangent_wide)
    grad_flat = projected_grad.astype(jnp.bfloat16).reshape(token_rows, 2 * features)
    normed_grad = lax.dot_general(
        grad_flat, weight, (((1,), (1,)), ((), ())), preferred_element_type=jnp.float32
    )
    frames_back, gain_in_grad = head_back(normed_grad.reshape(utterances, length, features))
    frame_grads = (cotangent_wide + frames_back).astype(jnp.bfloat16)
    owned_rows = lax.psum_scatter(
        lax.dot_general(
            jnp.take(normed_flat, safe_rows, axis=1) * valid_mask[None, :],
            grad_flat,
            (((0,), (0,)), ((), ())),
            preferred_element_type=jnp.float32,
        ).astype(jnp.bfloat16),
        "fsdp",
        scatter_dimension=0,
        tiled=True,
    )
    weight_sum = lax.psum(owned_rows, "dp").astype(jnp.float32)
    gain_in_total, gain_mid_total, kernel_total = lax.psum(
        (gain_in_grad, gain_mid_grad, kernel_grad), ("dp", "fsdp")
    )
    weight_grads = weight_sum.astype(jnp.bfloat16)
    return (frame_grads, weight_grads, gain_in_total, gain_mid_total, kernel_total)


def solution(mesh):
    in_specs = (
        P(("dp", "fsdp"), None, None),
        P(("dp", "fsdp"), None, None),
        P(("dp", "fsdp")),
        P("fsdp", None),
        P(),
        P(),
        P(),
        P(),
    )
    out_specs = (P(("dp", "fsdp"), None, None), P("fsdp", None), P(), P(), P())
    return jax.shard_map(
        per_device, mesh=mesh, in_specs=in_specs, out_specs=out_specs, check_vma=False
    )
```

profile of v0, /device:TPU:2, one launch (start us, length us, event | category | flops | bytes accessed | tf_op | source)
XLA Modules:
  0.0 746.2 jit_solution(6646918404065023754)
XLA Ops:
  7.2 0.0 copy-start
  7.2 0.0 copy-start.12
  7.2 0.0 all-gather.2.cloned.1.call-start
  7.2 0.7 all-gather.2.cloned.1.call-update
  7.9 0.0 reduce-scatter.2.cloned.1.call-start
  8.6 1.3 convert_reduce_fusion
  10.0 0.0 copy-start.18
  10.0 0.3 fusion.14
  10.3 0.6 copy-done.24
  10.9 0.0 copy-start.13
  10.9 0.3 fusion.25
  11.3 0.3 copy.13
  11.5 0.1 copy-done.13
  11.7 0.0 copy-start.11
  11.7 7.4 gather_fusion.1
  19.1 9.0 %scatter_custom_fusion = s32[1536]{0:T(1024)S(1)} fusion(s32[2304]{0:T(1024)S(1)} %get-tuple-element.117, s32[2304]{0:T(1024)S(1)} %iota.9, s32[]{:T(128)} %constant.48.clone.1), kind=kCustom, calls=%fused_computation.195 | custom fusion | bytes 6148 | tf_op jit(solution)/shard_map/scatter | solution.py:49
  28.1 0.0 copy-start.22
  28.1 0.0 copy-done.11
  28.1 0.2 slice_reduce_fusion.29
  28.4 0.3 slice_reduce_fusion.31
  28.7 0.0 copy-start.26
  28.7 86.9 %all-gather.2.cloned.1.call-done = bf16[2304,3072]{1,0:T(8,128)(2,1)} async-done(((bf16[144,3072]{1,0:T(8,128)(2,1)}), bf16[2304,3072]{1,0:T(8,128)(2,1)}) %all-gather.2.cloned.1.call-update) | async-done | bytes 14155792 | tf_op jit(solution)/shard_map/all_gather | solution.py:45
  115.7 24.8 %gather_fusion = bf16[1536,3072]{1,0:T(8,128)(2,1)} fusion(bf16[2304,3072]{1,0:T(8,128)(2,1)} %all-gather.2.cloned.1.call-done, s32[2048]{0:T(1024)S(1)} %pad_clamp_fusion.1), kind=kCustom, calls=%fused_computation | custom fusion | bytes 18880512 | tf_op jit(solution)/shard_map/jit(_take)/gather | solution.py:51
  140.5 0.0 copy-done.26
  140.5 6.4 convolution_bitcast_fusion
  146.9 0.4 multiply_multiply_fusion
  147.3 1.2 copy-done.2
  148.6 8.2 %fusion.44 = (f32[256]{0:T(256)S(1)}, f32[1,256,1536]{2,1,0:T(8,128)S(1)}) fusion(f32[1536]{0:T(1024)S(1)} %get-tuple-element.41, f32[1536]{0:T(1024)S(1)} %get-tuple-element.71, f32[1536]{0:T(1024)S(1)} %get-tuple-element.72, f32[1536]{0:T(1024)S(1)} %get-tuple-element.42, f32[1536]{0:T(1024)S(1)} %get-tuple-element.43, f32[1536]{0:T(1024)S(1)} %get-tuple-element.44, ...), kind=kLoop, calls=%fused_computation.216 | loop fusion | flops 25165568 | bytes 3343360 | tf_op jit(solution)/shard_map/jvp()/reduce_sum | solution.py:10
  156.7 0.0 copy-start.8
  156.7 0.0 copy-start.14
  156.8 0.3 multiply_reduce_fusion.34
  157.1 0.8 copy-done.8
  157.9 0.0 copy-done.14
  157.9 1.8 multiply_reduce_fusion.32
  159.6 0.5 fusion.42
  160.2 0.0 copy-start.16
  160.2 4.2 multiply_reduce_fusion.30
  164.4 9.1 %broadcast_multiply_fusion.31 = (f32[1,256,1536]{2,1,0:T(8,128)}, f32[1,256,1536]{2,1,0:T(8,128)}, f32[1,256,1536]{2,1,0:T(8,128)}, f32[1,256,1536]{2,1,0:T(8,12...) fusion(f32[1536]{0:T(1024)S(1)} %get-tuple-element.41, ...), kind=kLoop, calls=%fused_computation.149 | loop fusion | flops 7077888 | bytes 28417024 | tf_op jit(solution)/shard_map/transpose(jvp())/mul | solution.py:29
  173.5 7.2 broadcast_multiply_fusion
  180.7 14.8 %pad_add_fusion = f32[1,287,1536]{2,1,0:T(8,128)S(1)} fusion(f32[1,256,1536]{2,1,0:T(8,128)} %get-tuple-element.86, f32[1,256,1536]{2,1,0:T(8,128)} %get-tuple-element.87, f32[1,256,1536]{2,1,0:T(8,128)} %get-tuple-element.88, f32[1,256,1536]{2,1,0:T(8,128)} %get-tuple-element.89, f32[1,256,1536]{2,1,0:T(8,128)} %get-tuple-element.90, ...), kind=kLoop, calls=%fused_computation.24 | loop fusion | flops 11020800 | bytes 42657792 | tf_op jit(solution)/shard_map/transpose(jvp())/add_any | solution.py:29
  195.5 4.9 fusion.16
  200.5 0.4 fusion.40
  200.9 0.8 copy-done.4
  201.7 0.4 copy-done.6
  202.1 0.5 copy-done.7
  202.6 7.9 %convolution_convert_fusion = bf16[2304,3072]{1,0:T(8,128)(2,1)} fusion(bf16[2304,256]{1,0:T(8,128)(2,1)S(1)} %copy-done.7, pred[2304]{0:T(1024)(128)(4,1)S(1)} %get-tuple-element.115, bf16[2304]{0:T(1024)(128)(2,1)S(1)} %get-tuple-element.114, f32[1,256,1536]{2,1,0:T(8,128)S(1)} %fusion.40, f32[1,256,1536]{2,1,0:T(8,128)S(1)} %get-tuple-element.75), kind=kOutput, calls=%fused_computation.3 | convolution fusion | flops 3633709056 | bytes 18488064 | tf_op jit(solution)/shard_map/dot_general | solution.py:68
  210.5 0.0 reduce-scatter.2.cloned.1.call-update
  210.6 0.0 all-reduce.73.cloned.1.call-start
  210.8 0.4 copy-done.17
  211.2 5.0 multiply_reduce_fusion.31
  216.5 1.0 pad_add_fusion.7
  217.5 8.3 %fusion.15 = (f32[256]{0:T(256)S(1)}, f32[256,1536]{1,0:T(8,128)S(1)}) fusion(bf16[1,256,1536]{2,1,0:T(8,128)(2,1)} %param.8, f32[1536]{0:T(1024)S(1)} %copy-done.12, f32[256]{0:T(256)S(1)} %copy-done.19, bf16[1536,3072]{1,0:T(8,128)(2,1)} %gather_fusion, pred[1536]{0:T(1024)(128)(4,1)S(1)} %copy-done.27, f32[1,256,1536]{2,1,0:T(8,128)} %copy-done.6, ...), kind=kOutput, calls=%fused_computation.62 | convolution fusion | flops 2424176384 | bytes 14951936 | tf_op jit(solution)/shard_map/dot_general | solution.py:62
  225.8 0.0 copy-start.1
  225.8 0.0 all-reduce.73.cloned.1.call-update
  225.9 0.0 all-reduce.71.cloned.1.call-start
  225.9 120.1 %reduce-scatter.2.cloned.1.call-done = bf16[144,3072]{1,0:T(8,128)(2,1)} async-done(((bf16[2304,3072]{1,0:T(8,128)(2,1)}), bf16[144,3072]{1,0:T(8,128)(2,1)}) %reduce-scatter.2.cloned.1.call-update) | async-done | bytes 884752 | tf_op jit(solution)/shard_map/reduce_scatter | solution.py:67
  346.0 0.0 all-reduce.71.cloned.1.call-update
  346.1 0.8 fusion.10
  346.9 74.4 %all-reduce.67 = (f32[1536]{0:T(1024)}, f32[1536]{0:T(1024)}) all-reduce(f32[1536]{0:T(1024)S(1)} %get-tuple-element.39, f32[1536]{0:T(1024)S(1)} %copy-done.15), channel_id=1, replica_groups=mesh['dp'=16,'fsdp'=16] {'dp','fsdp'}, use_global_device_ids=true, to_apply=%region_12.13 | all-reduce | flops 3072 | bytes 24576 | tf_op jit(solution)/shard_map/psum | solution.py:79
  421.3 1.5 fusion.13
  422.8 175.4 %all-reduce.73.cloned.1.call-done = f32[32,1536]{1,0:T(8,128)} async-done(((f32[32,1536]{1,0:T(8,128)}), f32[32,1536]{1,0:T(8,128)}) %all-reduce.73.cloned.1.call-update) | async-done | bytes 196624 | tf_op jit(solution)/shard_map/psum | solution.py:79
  598.2 138.6 %all-reduce.71.cloned.1.call-done = bf16[144,3072]{1,0:T(8,128)(2,1)} async-done(((bf16[144,3072]{1,0:T(8,128)(2,1)}), bf16[144,3072]{1,0:T(8,128)(2,1)}) %all-reduce.71.cloned.1.call-update) | async-done | bytes 884752 | tf_op jit(solution)/shard_map/psum | solution.py:78
  736.8 2.1 copy.17
  738.9 0.7 copy.18
  (82 shorter events, 0.4 us)
Async XLA Ops:
  7.2 2.8 copy-start
  7.2 3.7 copy-start.12
  7.2 108.5 %all-gather.2.cloned.1.call-start = ((), (), s32[]{:S(2)}) async-start(), calls=%async_computation.1 | async-start | bytes 15040512 | tf_op jit(solution)/shard_map/all_gather | solution.py:45
  7.9 338.1 %reduce-scatter.2.cloned.1.call-start = ((), (), s32[]{:S(2)}) async-start(), calls=%async_computation.2 | async-start | bytes 15040512 | tf_op jit(solution)/shard_map/reduce_scatter | solution.py:67
  10.0 1.6 copy-start.18
  10.3 0.6 copy-start.24
  10.9 0.6 copy-start.20
  10.9 0.7 copy-start.13
  11.7 16.5 %copy-start.11 = (f32[32,1536]{1,0:T(8,128)S(1)}, f32[32,1536]{1,0:T(8,128)}, u32[]{:S(2)}) copy-start(f32[32,1536]{1,0:T(8,128)} %param.15) | copy-start | bytes 589828
  28.1 129.0 %copy-start.22 = (f32[256]{0:T(256)}, f32[256]{0:T(256)S(1)}, u32[]{:S(2)}) copy-start(f32[256]{0:T(256)S(1)} %compare_convert_fusion.1) | copy-start | bytes 3076
  28.7 111.8 %copy-start.26 = (pred[1536]{0:T(1024)(128)(4,1)}, pred[1536]{0:T(1024)(128)(4,1)S(1)}, u32[]{:S(2)}) copy-start(pred[1536]{0:T(1024)(128)(4,1)S(1)} %compare_and_fusion.1) | copy-start | bytes 4612
  146.9 1.7 copy-start.2
  156.7 1.1 copy-start.8
  156.7 1.1 copy-start.14
  160.2 13.3 %copy-start.16 = (f32[256]{0:T(256)}, f32[256]{0:T(256)S(1)}, u32[]{:S(2)}) copy-start(f32[256]{0:T(256)S(1)} %negate_multiply_fusion.1) | copy-start | bytes 3076
  180.7 14.8 %copy-start.3 = (f32[1,256,3072]{2,1,0:T(8,128)S(1)}, f32[1,256,3072]{2,1,0:T(8,128)}, u32[]{:S(2)}) copy-start(f32[1,256,3072]{2,1,0:T(8,128)} %copy-done.2) | copy-start | bytes 9437188
  180.7 14.8 %copy-start.5 = (f32[1,256,1536]{2,1,0:T(8,128)S(1)}, f32[1,256,1536]{2,1,0:T(8,128)}, u32[]{:S(2)}) copy-start(f32[1,256,1536]{2,1,0:T(8,128)} %get-tuple-element.85) | copy-start | bytes 4718596
  180.7 14.8 %copy-start.23 = (f32[256]{0:T(256)S(1)}, f32[256]{0:T(256)}, u32[]{:S(2)}) copy-start(f32[256]{0:T(256)} %copy-done.22) | copy-start | bytes 3076
  200.4 1.2 copy-start.4
  200.5 2.1 copy-start.7
  200.9 1.2 copy-start.6
  210.5 0.7 copy-start.17
  210.6 387.6 %all-reduce.73.cloned.1.call-start = ((), (), s32[]{:S(2)}) async-start(), calls=%async_computation.4 | async-start | bytes 393216 | tf_op jit(solution)/shard_map/psum | solution.py:79
  211.2 6.3 copy-start.19
  211.2 6.3 copy-start.27
  217.5 8.4 %copy-start.25 = (f32[256]{0:T(256)S(1)}, f32[256]{0:T(256)}, u32[]{:S(2)}) copy-start(f32[256]{0:T(256)} %copy-done.24) | copy-start | bytes 3076
  217.5 128.5 %copy-start.21 = (f32[256]{0:T(256)S(1)}, f32[256]{0:T(256)}, u32[]{:S(2)}) copy-start(f32[256]{0:T(256)} %copy-done.20) | copy-start | bytes 3076
  225.8 120.2 %copy-start.1 = (bf16[1,256,1536]{2,1,0:T(8,128)(2,1)S(1)}, bf16[1,256,1536]{2,1,0:T(8,128)(2,1)}, u32[]{:S(2)}) copy-start(bf16[1,256,1536]{2,1,0:T(8,128)(2,1)} %param.8) | copy-start | bytes 2359300
  225.9 510.9 %all-reduce.71.cloned.1.call-start = ((), (), s32[]{:S(2)}) async-start(), calls=%async_computation.3 | async-start | bytes 1769472 | tf_op jit(solution)/shard_map/psum | solution.py:78
  346.0 0.8 copy-start.15
  346.0 75.3 %copy-start.9 = (bf16[1,256,1536]{2,1,0:T(8,128)(2,1)S(1)}, bf16[1,256,1536]{2,1,0:T(8,128)(2,1)}, u32[]{:S(2)}) copy-start(bf16[1,256,1536]{2,1,0:T(8,128)(2,1)} %param.9) | copy-start | bytes 2359300
  598.2 140.8 %copy-start.10 = (f32[32,1536]{1,0:T(8,128)S(1)}, f32[32,1536]{1,0:T(8,128)}, u32[]{:S(2)}) copy-start(f32[32,1536]{1,0:T(8,128)} %all-reduce.73.cloned.1.call-done) | copy-start | bytes 589828
Sparse Core Ops, SparseCore 0:
  10.7 104.8 all-gather.1
  210.7 135.3 reduce-scatter.1
  353.0 245.1 all-reduce.72
  600.9 135.8 all-reduce.70
where the time goes:
time: 747 us; the launch traced here: 746 us
  waiting for transfers between devices  522 us (70%)
  blocking collectives  74.4 us (10%)
  other arithmetic  62.2 us (8%)
  local copies, waits for them, and re-layouts  49.9 us (7%)
  matrix products  22.6 us (3%)
  between operations  15.1 us (2%)
    psum x1, waiting for transfers between devices, per_device(): lax.psum((gain_in_grad, gain_mid_grad, kernel_grad), ('dp', 'fsdp'))  175 us
    psum x1, waiting for transfers between devices, per_device(): weight_sum = lax.psum(owned_rows, 'dp').astype(jnp.float32)  139 us
    reduce_scatter x1, waiting for transfers between devices, per_device(): lax.psum_scatter(lax.dot_general(jnp.take(normed_flat, safe_rows, axis=1)...  120 us
    all_gather x1, waiting for transfers between devices, per_device(): gathered = lax.all_gather(weight_slots, 'fsdp', axis=0, tiled=True)  86.9 us
    psum x1, blocking collectives, per_device(): lax.psum((gain_in_grad, gain_mid_grad, kernel_grad), ('dp', 'fsdp'))  74.4 us
    gather x1, local copies, waits for them, and re-layouts, per_device(): weight = jnp.take(gathered, inverse, axis=0)  24.8 us
    mul x2, other arithmetic, branch_tail(): kernel[offset] * padded[:, offset:offset + length, :]  16.3 us
  transfers between devices with their start and end apart: 4, of which 4 were waited for; matrix products, arithmetic and copies ran while one was open for 5% of the time, Pallas kernels for 0%

commit v1 on v0

--- a/solution.py
+++ b/solution.py
@@ -75,7 +75,7 @@
         scatter_dimension=0,
         tiled=True,
     )
-    weight_sum = lax.psum(owned_rows, "dp").astype(jnp.float32)
+    weight_sum = jnp.sum(jax.lax.all_gather(owned_rows, "dp"), axis=0).astype(jnp.float32)
     gain_in_total, gain_mid_total, kernel_total = lax.psum(
         (gain_in_grad, gain_mid_grad, kernel_grad), ("dp", "fsdp")
     )

time: 747 us -> 772 us (1.033)
  blocking collectives: 74.4 us -> 209 us
  waiting for transfers between devices: 522 us -> 399 us
  other arithmetic: 62.2 us -> 72.7 us
    psum x1 -> x0, waiting for transfers between devices: 139 us -> none  [per_device(): weight_sum = lax.psum(owned_rows, 'dp').astype(jnp.float32)]
    psum x1, blocking collectives: 74.4 us -> 209 us  [per_device(): lax.psum((gain_in_grad, gain_mid_grad, kernel_grad), ('dp', 'fsdp'))]
    reduce_scatter x1, waiting for transfers between devices: 120 us -> 135 us  [per_device(): lax.psum_scatter(lax.dot_general(jnp.take(normed_flat, safe_rows, axis=1)...]
    reduce_sum x0 -> x1, other arithmetic: none -> 9.28 us  [per_device(): jnp.sum(jax.lax.all_gather(owned_rows, 'dp'), axis=0).astype(jnp.float32)]
  transfers between devices with their start and end apart: 4 -> 4, of which waited for: 4 -> 3; matrix products, arithmetic and copies ran while one was open for 5% -> 6% of each run, Pallas kernels for 0% -> 0%
where the time goes in v1:
time: 772 us; the launch traced here: 767 us
  waiting for transfers between devices  399 us (52%)
  blocking collectives  209 us (27%)
  other arithmetic  72.7 us (9%)
  local copies, waits for them, and re-layouts  49.4 us (6%)
  matrix products  20.9 us (3%)
  between operations  15.4 us (2%)
    psum x1, blocking collectives, per_device(): lax.psum((gain_in_grad, gain_mid_grad, kernel_grad), ('dp', 'fsdp'))  209 us
    psum x1, waiting for transfers between devices, per_device(): lax.psum((gain_in_grad, gain_mid_grad, kernel_grad), ('dp', 'fsdp'))  177 us
    reduce_scatter x1, waiting for transfers between devices, per_device(): lax.psum_scatter(lax.dot_general(jnp.take(normed_flat, safe_rows, axis=1)...  135 us
    all_gather x1, waiting for transfers between devices, per_device(): gathered = lax.all_gather(weight_slots, 'fsdp', axis=0, tiled=True)  86.2 us
    gather x1, local copies, waits for them, and re-layouts, per_device(): weight = jnp.take(gathered, inverse, axis=0)  25.1 us
    mul x2, other arithmetic, branch_tail(): kernel[offset] * padded[:, offset:offset + length, :]  17 us
  transfers between devices with their start and end apart: 4, of which 3 were waited for; matrix products, arithmetic and copies ran while one was open for 6% of the time, Pallas kernels for 0%

profile of v1, /device:TPU:2, one launch (start us, length us, event | category | flops | bytes accessed | tf_op | source)
XLA Modules:
  0.0 766.7 jit_solution(7691299890900381354)
XLA Ops:
  7.2 0.0 copy-start
  7.2 0.0 all-gather.4.cloned.1.call-start
  7.2 0.7 all-gather.4.cloned.1.call-update
  7.9 0.0 reduce-scatter.2.cloned.1.call-start
  8.6 1.3 convert_reduce_fusion
  10.0 0.0 copy-start.18
  10.0 0.3 fusion.14
  10.3 0.6 copy-done.24
  10.9 0.0 copy-start.13
  10.9 0.3 fusion.25
  11.3 0.3 copy-done.20
  11.5 0.3 copy.13
  11.8 0.0 copy-start.11
  11.8 7.4 gather_fusion.1
  19.3 9.0 %scatter_custom_fusion = s32[1536]{0:T(1024)S(1)} fusion(s32[2304]{0:T(1024)S(1)} %get-tuple-element.117, s32[2304]{0:T(1024)S(1)} %iota.9, s32[]{:T(128)} %constant.49.clone.1), kind=kCustom, calls=%fused_computation.195 | custom fusion | bytes 6148 | tf_op jit(solution)/shard_map/scatter | solution.py:49
  28.3 0.0 copy-start.22
  28.3 0.2 slice_reduce_fusion.29
  28.5 0.3 slice_reduce_fusion.31
  28.9 0.0 copy-start.26
  28.9 0.6 compare_convert_fusion
  29.5 86.2 %all-gather.4.cloned.1.call-done = bf16[2304,3072]{1,0:T(8,128)(2,1)} async-done(((bf16[144,3072]{1,0:T(8,128)(2,1)}), bf16[2304,3072]{1,0:T(8,128)(2,1)}) %all-gather.4.cloned.1.call-update) | async-done | bytes 14155792 | tf_op jit(solution)/shard_map/all_gather | solution.py:45
  115.7 25.1 %gather_fusion = bf16[1536,3072]{1,0:T(8,128)(2,1)} fusion(bf16[2304,3072]{1,0:T(8,128)(2,1)} %all-gather.4.cloned.1.call-done, s32[2048]{0:T(1024)S(1)} %pad_clamp_fusion.1), kind=kCustom, calls=%fused_computation | custom fusion | bytes 18880512 | tf_op jit(solution)/shard_map/jit(_take)/gather | solution.py:51
  140.8 6.4 convolution_bitcast_fusion
  147.2 0.4 multiply_multiply_fusion
  147.6 1.2 copy-done.3
  148.8 8.1 %fusion.44 = (f32[256]{0:T(256)S(1)}, f32[1,256,1536]{2,1,0:T(8,128)S(1)}) fusion(f32[1536]{0:T(1024)S(1)} %get-tuple-element.41, f32[1536]{0:T(1024)S(1)} %get-tuple-element.71, f32[1536]{0:T(1024)S(1)} %get-tuple-element.72, f32[1536]{0:T(1024)S(1)} %get-tuple-element.42, f32[1536]{0:T(1024)S(1)} %get-tuple-element.43, f32[1536]{0:T(1024)S(1)} %get-tuple-element.44, ...), kind=kLoop, calls=%fused_computation.216 | loop fusion | flops 25165568 | bytes 3343360 | tf_op jit(solution)/shard_map/jvp()/reduce_sum | solution.py:10
  157.0 0.0 copy-start.9
  157.0 0.0 copy-start.14
  157.0 0.3 multiply_reduce_fusion.34
  157.3 0.8 copy-done.9
  158.1 1.2 multiply_reduce_fusion.32
  159.4 0.5 fusion.42
  159.9 0.0 copy-start.16
  159.9 0.6 copy-done.16
  160.4 4.3 multiply_reduce_fusion.30
  164.8 0.0 copy-start.17
  164.8 9.8 %broadcast_multiply_fusion.31 = (f32[1,256,1536]{2,1,0:T(8,128)}, f32[1,256,1536]{2,1,0:T(8,128)}, f32[1,256,1536]{2,1,0:T(8,128)}, f32[1,256,1536]{2,1,0:T(8,12...) fusion(f32[1536]{0:T(1024)S(1)} %get-tuple-element.41, ...), kind=kLoop, calls=%fused_computation.149 | loop fusion | flops 7077888 | bytes 28417024 | tf_op jit(solution)/shard_map/transpose(jvp())/mul | solution.py:29
  174.6 7.2 broadcast_multiply_fusion
  181.8 14.8 %pad_add_fusion = f32[1,287,1536]{2,1,0:T(8,128)S(1)} fusion(f32[1,256,1536]{2,1,0:T(8,128)} %get-tuple-element.86, f32[1,256,1536]{2,1,0:T(8,128)} %get-tuple-element.87, f32[1,256,1536]{2,1,0:T(8,128)} %get-tuple-element.88, f32[1,256,1536]{2,1,0:T(8,128)} %get-tuple-element.89, f32[1,256,1536]{2,1,0:T(8,128)} %get-tuple-element.90, ...), kind=kLoop, calls=%fused_computation.24 | loop fusion | flops 11020800 | bytes 42657792 | tf_op jit(solution)/shard_map/transpose(jvp())/add_any | solution.py:29
  196.6 5.4 fusion.16
  202.0 0.0 copy-start.15
  202.0 0.4 fusion.40
  202.4 0.8 copy-done.5
  203.2 0.4 copy-done.7
  203.6 0.5 copy-done.8
  204.1 7.9 %convolution_convert_fusion = bf16[2304,3072]{1,0:T(8,128)(2,1)} fusion(bf16[2304,256]{1,0:T(8,128)(2,1)S(1)} %copy-done.8, pred[2304]{0:T(1024)(128)(4,1)S(1)} %copy-done.15, bf16[2304]{0:T(1024)(128)(2,1)S(1)} %get-tuple-element.114, f32[1,256,1536]{2,1,0:T(8,128)S(1)} %fusion.40, f32[1,256,1536]{2,1,0:T(8,128)S(1)} %get-tuple-element.75), kind=kOutput, calls=%fused_computation.3 | convolution fusion | flops 3633709056 | bytes 18488064 | tf_op jit(solution)/shard_map/dot_general | solution.py:68
  212.1 0.0 reduce-scatter.2.cloned.1.call-update
  212.1 0.0 all-gather.6.cloned.1.call-start
  212.1 135.4 %reduce-scatter.2.cloned.1.call-done = bf16[144,3072]{1,0:T(8,128)(2,1)} async-done(((bf16[2304,3072]{1,0:T(8,128)(2,1)}), bf16[144,3072]{1,0:T(8,128)(2,1)}) %reduce-scatter.2.cloned.1.call-update) | async-done | bytes 884752 | tf_op jit(solution)/shard_map/reduce_scatter | solution.py:67
  347.6 0.0 all-gather.6.cloned.1.call-update
  347.6 0.0 all-reduce.70.cloned.1.call-start
  347.9 0.0 copy-start.1
  347.9 0.0 copy-start.27
  347.9 5.0 multiply_reduce_fusion.31
  353.2 6.6 fusion.15
  359.9 0.0 copy-start.10
  359.9 0.8 fusion.10
  360.7 1.0 pad_add_fusion.7
  361.7 0.0 all-reduce.70.cloned.1.call-update
  361.8 1.5 fusion.13
  363.3 209.2 %all-reduce.67 = (f32[1536]{0:T(1024)}, f32[1536]{0:T(1024)}) all-reduce(f32[1536]{0:T(1024)S(1)} %get-tuple-element.39, f32[1536]{0:T(1024)S(1)} %get-tuple-element.37), channel_id=1, replica_groups=mesh['dp'=16,'fsdp'=16] {'dp','fsdp'}, use_global_device_ids=true, to_apply=%region_12.13 | all-reduce | flops 3072 | bytes 24576 | tf_op jit(solution)/shard_map/psum | solution.py:79
  572.5 9.3 %reduce_sum.394 = bf16[144,3072]{1,0:T(8,128)(2,1)} reduce(bf16[16,144,3072]{2,1,0:T(8,128)(2,1)} %bitcast.24, bf16[]{:T(256)} %constant.57.clone.1), dimensions={0}, to_apply=%region_10.11 | reduce | flops 6635520 | bytes 15040514 | tf_op jit(solution)/shard_map/reduce_sum | solution.py:78
  581.8 176.6 %all-reduce.70.cloned.1.call-done = f32[32,1536]{1,0:T(8,128)} async-done(((f32[32,1536]{1,0:T(8,128)}), f32[32,1536]{1,0:T(8,128)}) %all-reduce.70.cloned.1.call-update) | async-done | bytes 196624 | tf_op jit(solution)/shard_map/psum | solution.py:79
  758.3 1.6 copy.16
  (82 shorter events, 0.4 us)
Async XLA Ops:
  7.2 2.8 copy-start
  7.2 3.7 copy-start.12
  7.2 108.5 %all-gather.4.cloned.1.call-start = ((), (), s32[]{:S(2)}) async-start(), calls=%async_computation.1 | async-start | bytes 15040512 | tf_op jit(solution)/shard_map/all_gather | solution.py:45
  7.9 339.7 %reduce-scatter.2.cloned.1.call-start = ((), (), s32[]{:S(2)}) async-start(), calls=%async_computation.2 | async-start | bytes 15040512 | tf_op jit(solution)/shard_map/reduce_scatter | solution.py:67
  10.0 1.3 copy-start.18
  10.3 0.6 copy-start.24
  10.9 0.6 copy-start.20
  10.9 0.9 copy-start.13
  11.8 16.5 %copy-start.11 = (f32[32,1536]{1,0:T(8,128)S(1)}, f32[32,1536]{1,0:T(8,128)}, u32[]{:S(2)}) copy-start(f32[32,1536]{1,0:T(8,128)} %param.15) | copy-start | bytes 589828
  28.3 129.0 %copy-start.22 = (f32[256]{0:T(256)}, f32[256]{0:T(256)S(1)}, u32[]{:S(2)}) copy-start(f32[256]{0:T(256)S(1)} %compare_convert_fusion.1) | copy-start | bytes 3076
  28.9 111.9 %copy-start.26 = (pred[1536]{0:T(1024)(128)(4,1)}, pred[1536]{0:T(1024)(128)(4,1)S(1)}, u32[]{:S(2)}) copy-start(pred[1536]{0:T(1024)(128)(4,1)S(1)} %compare_and_fusion.1) | copy-start | bytes 4612
  147.2 1.7 copy-start.3
  157.0 1.1 copy-start.9
  157.0 1.1 copy-start.14
  159.9 0.6 copy-start.16
  164.8 9.8 %copy-start.17 = (f32[256]{0:T(256)S(1)}, f32[256]{0:T(256)}, u32[]{:S(2)}) copy-start(f32[256]{0:T(256)} %copy-done.16) | copy-start | bytes 3076
  181.8 14.8 %copy-start.4 = (f32[1,256,3072]{2,1,0:T(8,128)S(1)}, f32[1,256,3072]{2,1,0:T(8,128)}, u32[]{:S(2)}) copy-start(f32[1,256,3072]{2,1,0:T(8,128)} %copy-done.3) | copy-start | bytes 9437188
  181.8 14.8 %copy-start.23 = (f32[256]{0:T(256)S(1)}, f32[256]{0:T(256)}, u32[]{:S(2)}) copy-start(f32[256]{0:T(256)} %copy-done.22) | copy-start | bytes 3076
  202.0 1.2 copy-start.5
  202.0 2.1 copy-start.8
  202.0 2.1 copy-start.15
  202.4 1.2 copy-start.7
  212.1 360.4 %all-gather.6.cloned.1.call-start = ((), (), s32[]{:S(2)}) async-start(), calls=%async_computation.4 | async-start | bytes 15040512 | tf_op jit(solution)/shard_map/all_gather | solution.py:78
  347.6 410.7 %all-reduce.70.cloned.1.call-start = ((), (), s32[]{:S(2)}) async-start(), calls=%async_computation.3 | async-start | bytes 393216 | tf_op jit(solution)/shard_map/psum | solution.py:79
  347.9 5.3 copy-start.1
  347.9 5.3 copy-start.6
  347.9 5.3 copy-start.19
  347.9 5.3 copy-start.27
  353.2 6.7 copy-start.25
  353.2 6.7 copy-start.21
  359.8 1.9 copy-start.2
  359.9 1.9 copy-start.10
Sparse Core Ops, SparseCore 0:
  10.7 104.8 all-gather.3
  212.2 135.3 reduce-scatter.1
  349.5 158.1 all-gather.5
  514.6 243.7 all-reduce.69
